TPU v7x, 32 devices: a whole 2x2x4 slice. The times are simulated.
32 devices in a mesh: seq: 8 (over z, core), tp: 4 (over y, x).
Axes of the slice: x: 2, y: 2, z: 4, core: 2. Of those that a mesh axis runs over, the one named last changes fastest.
Arguments:
- layer_in: bfloat16 [4096, 2048], P('seq'), may hold values from -6 to 6
- positions: int32 [4096], P('seq'), may hold values from 0 to 2047, as said below
- seq_ids: int32 [4096], P('seq'), may hold values from 0 to 1, as said below
- norm1_gain: float32 [2048], replicated, may hold values from 0.5 to 1.5
- norm2_gain: float32 [2048], replicated, may hold values from 0.5 to 1.5
- w_query: float32 [2048, 2048], P('seq', 'tp'), may hold values from -0.125 to 0.125
- w_key: float32 [2048, 2048], P('seq', 'tp'), may hold values from -0.125 to 0.125
- w_value: float32 [2048, 2048], P('seq', 'tp'), may hold values from -0.125 to 0.125
- w_out: float32 [2048, 2048], P('tp', 'seq'), may hold values from -4 to 4
- w_gate: float32 [2048, 8192], P('seq', 'tp'), may hold values from -0.125 to 0.125
- w_up: float32 [2048, 8192], P('seq', 'tp'), may hold values from -0.125 to 0.125
- w_down: float32 [8192, 2048], P('tp', 'seq'), may hold values from -0.0625 to 0.0625
- out_grad: bfloat16 [4096, 2048], P('seq'), may hold values from -6 to 6
Outputs:
- layer_out: bfloat16 [4096, 2048], P('seq')
- in_grad: float32 [4096, 2048], P('seq')
- grad_norm1: float32 [2048], P('seq')
- grad_norm2: float32 [2048], P('seq')
- grad_w_query: float32 [2048, 2048], P('seq', 'tp')
- grad_w_key: float32 [2048, 2048], P('seq', 'tp')
- grad_w_value: float32 [2048, 2048], P('seq', 'tp')
- grad_w_out: float32 [2048, 2048], P('tp', 'seq')
- grad_w_gate: float32 [2048, 8192], P('seq', 'tp')
- grad_w_up: float32 [2048, 8192], P('seq', 'tp')
- grad_w_down: float32 [8192, 2048], P('tp', 'seq')
Inputs may be any that keep to these rules, and one draw needn't show every extreme that they name: The shard of 512 rows at index r of seq holds, in an order that varies from shard to shard, four blocks of 128 consecutive positions: for each of the two sequences its blocks number r and 15 - r. Each position of each sequence appears once. `seq_ids`: the sequence of each row, constant over each block of 128 rows described for positions; each shard holds two such blocks of each sequence, and each sequence has 2048 rows.
All inputs are finite; a program needn't handle non-finite values.
Results may differ from a plain program's by a relative error of at most 0.024.
Values may be sent and summed in bfloat16 or wider, within the bound.
No kernel may reach another device: no remote copies, remote signals or barrier semaphores. Data moves between devices by JAX's collectives and lax.ppermute only.
A program may use at most 192 MiB of HBM per device.

v0:
```python
import math
import jax
import jax.numpy as jnp
from jax import lax
from jax.sharding import PartitionSpec as P

HD = 128
EPSILON = 1e-06


def angles(places):
    half_width = HD // 2
    frequency = jnp.power(
        jnp.float32(10000.0), -jnp.arange(half_width, dtype=jnp.float32) / half_width
    )
    phase_angle = places.astype(jnp.float32)[:, None] * frequency[None, :]
    return (jnp.cos(phase_angle)[:, None, :], jnp.sin(phase_angle)[:, None, :])


def rotate(heads, rot_cos, rot_sin):
    half_width = heads.shape[-1] // 2
    front_half = heads[..., :half_width]
    back_half = heads[..., half_width:]
    return jnp.concatenate(
        [front_half * rot_cos - back_half * rot_sin, back_half * rot_cos + front_half * rot_sin],
        axis=-1,
    )


def rotate_back(grads, rot_cos, rot_sin):
    half_width = grads.shape[-1] // 2
    front_half = grads[..., :half_width]
    back_half = grads[..., half_width:]
    return jnp.concatenate(
        [front_half * rot_cos + back_half * rot_sin, back_half * rot_cos - front_half * rot_sin],
        axis=-1,
    )


def matrix(left, right):
    return jnp.dot(left, right, preferred_element_type=jnp.float32)


def inner_rows(left, right):
    return lax.dot_general(
        left, right, (((0,), (0,)), ((), ())), preferred_element_type=jnp.float32
    )


def outer_cols(left, right):
    return lax.dot_general(
        left, right, (((1,), (1,)), ((), ())), preferred_element_type=jnp.float32
    )


def arrange(values, order):
    blocks = values.reshape((4, values.shape[0] // 4) + values.shape[1:])
    return blocks[order].reshape(values.shape)


def regroup(values, shard_rows):
    count = values.shape[0] // shard_rows
    half_rows = shard_rows // 2
    split_form = values.reshape((count, 2, half_rows) + values.shape[1:])
    return jnp.swapaxes(split_form, 0, 1).reshape((2, count * half_rows) + values.shape[1:])


def unsplit(values):
    return values.reshape((values.shape[0] * values.shape[1],) + values.shape[2:])


def split_scores(query_split, key_split, qpos_split, kpos_split, score_scale, score_bias):
    raw = (
        jnp.einsum("sqhd,skhd->shqk", query_split, key_split, preferred_element_type=jnp.float32)
        * score_scale
        + score_bias
    )
    allowed = (kpos_split[:, None, :] <= qpos_split[:, :, None])[:, None]
    return (jax.nn.sigmoid(raw), allowed)


def split_attend(
    query_split, key_split, value_split, qpos_split, kpos_split, score_scale, score_bias
):
    sig, allowed = split_scores(
        query_split, key_split, qpos_split, kpos_split, score_scale, score_bias
    )
    attn_weights = jnp.where(allowed, sig, 0.0).astype(jnp.bfloat16)
    return unsplit(
        jnp.einsum("shqk,skhd->sqhd", attn_weights, value_split, preferred_element_type=jnp.float32)
    )


def split_grads(
    query_split, key_split, value_split, grad_split, qpos_split, kpos_split, score_scale, score_bias
):
    sig, allowed = split_scores(
        query_split, key_split, qpos_split, kpos_split, score_scale, score_bias
    )
    attn_weights = jnp.where(allowed, sig, 0.0).astype(jnp.bfloat16)
    grad_prob = jnp.einsum(
        "sqhd,skhd->shqk", grad_split, value_split, preferred_element_type=jnp.float32
    )
    grad_score = jnp.where(allowed, grad_prob * sig * (1.0 - sig), 0.0).astype(jnp.bfloat16)
    return (attn_weights, grad_score)


def on_device(
    layer_in,
    positions,
    seq_ids,
    norm1_gain,
    norm2_gain,
    w_query,
    w_key,
    w_value,
    w_out,
    w_gate,
    w_up,
    w_down,
    out_grad,
):
    row_count = layer_in.shape[0]
    shard_count = lax.axis_size("seq")
    score_bias = -math.log(shard_count * row_count // 2)
    score_scale = 1.0 / math.sqrt(HD)
    block_seq = seq_ids.reshape(4, row_count // 4)[:, 0]
    order = jnp.argsort(block_seq, stable=True)
    inverse = jnp.argsort(order, stable=True)
    pos_sorted = arrange(positions, order)
    seq_sorted = arrange(seq_ids, order)
    every_pos, every_seq = (
        lax.all_gather(pos_sorted, "seq", axis=0, tiled=True),
        lax.all_gather(seq_sorted, "seq", axis=0, tiled=True),
    )
    query_full, key_full, value_full, out_full, gate_full, up_full, down_full = (
        lax.all_gather(w_query.astype(jnp.bfloat16), "seq", axis=0, tiled=True),
        lax.all_gather(w_key.astype(jnp.bfloat16), "seq", axis=0, tiled=True),
        lax.all_gather(w_value.astype(jnp.bfloat16), "seq", axis=0, tiled=True),
        lax.all_gather(w_out.astype(jnp.bfloat16), "seq", axis=1, tiled=True),
        lax.all_gather(w_gate.astype(jnp.bfloat16), "seq", axis=0, tiled=True),
        lax.all_gather(w_up.astype(jnp.bfloat16), "seq", axis=0, tiled=True),
        lax.all_gather(w_down.astype(jnp.bfloat16), "seq", axis=1, tiled=True),
    )
    head_cols = query_full.shape[1]
    head_count = head_cols // HD
    rot_cos, rot_sin = angles(positions)
    inputs = layer_in.astype(jnp.float32)
    scale_one = lax.rsqrt(jnp.mean(inputs * inputs, axis=-1, keepdims=True) + EPSILON)
    normed_one = (inputs * scale_one * norm1_gain).astype(jnp.bfloat16)
    query_heads = rotate(
        matrix(normed_one, query_full).reshape(row_count, head_count, HD), rot_cos, rot_sin
    ).astype(jnp.bfloat16)
    key_heads = rotate(
        matrix(normed_one, key_full).reshape(row_count, head_count, HD), rot_cos, rot_sin
    ).astype(jnp.bfloat16)
    value_rows = matrix(normed_one, value_full).astype(jnp.bfloat16)
    query_sorted = arrange(query_heads, order)
    key_rows = arrange(key_heads.reshape(row_count, head_cols), order)
    value_sorted = arrange(value_rows, order)
    query_split = regroup(query_sorted, row_count)
    qpos_split = regroup(pos_sorted, row_count)
    zero_out = jnp.zeros((row_count, head_count, HD), jnp.float32)
    key_block = lax.all_gather(key_rows, "seq", axis=0, tiled=True)
    value_block = lax.all_gather(value_sorted, "seq", axis=0, tiled=True)
    piece_rows = key_block.shape[0]
    key_pos = every_pos
    key_heads_piece = key_block.reshape(piece_rows, head_count, HD)
    value_heads_piece = value_block.reshape(piece_rows, head_count, HD)
    term = split_attend(
        query_split,
        regroup(key_heads_piece, row_count),
        regroup(value_heads_piece, row_count),
        qpos_split,
        regroup(key_pos, row_count),
        score_scale,
        score_bias,
    )
    mixed_heads = arrange(term, inverse).reshape(row_count, head_cols).astype(jnp.bfloat16)
    residual = inputs + lax.psum(matrix(mixed_heads, out_full), "tp")
    scale_two = lax.rsqrt(jnp.mean(residual * residual, axis=-1, keepdims=True) + EPSILON)
    normed_two = (residual * scale_two * norm2_gain).astype(jnp.bfloat16)
    gate = matrix(normed_two, gate_full)
    up_proj = matrix(normed_two, up_full)
    gate_sig = jax.nn.sigmoid(gate)
    hidden = (gate * gate_sig * up_proj).astype(jnp.bfloat16)
    layer_out = (
        residual
        + lax.psum(matrix(hidden, down_full).astype(jnp.bfloat16), "tp").astype(jnp.float32)
    ).astype(jnp.bfloat16)
    query_full, key_full, value_full, out_full, gate_full, up_full, down_full = (
        lax.all_gather(w_query.astype(jnp.bfloat16), "seq", axis=0, tiled=True),
        lax.all_gather(w_key.astype(jnp.bfloat16), "seq", axis=0, tiled=True),
        lax.all_gather(w_value.astype(jnp.bfloat16), "seq", axis=0, tiled=True),
        lax.all_gather(w_out.astype(jnp.bfloat16), "seq", axis=1, tiled=True),
        lax.all_gather(w_gate.astype(jnp.bfloat16), "seq", axis=0, tiled=True),
        lax.all_gather(w_up.astype(jnp.bfloat16), "seq", axis=0, tiled=True),
        lax.all_gather(w_down.astype(jnp.bfloat16), "seq", axis=1, tiled=True),
    )
    grad_w_down = inner_rows(hidden, out_grad)
    grad_hidden = outer_cols(out_grad, down_full)
    grad_gate = (grad_hidden * up_proj * gate_sig * (1.0 + gate * (1.0 - gate_sig))).astype(
        jnp.bfloat16
    )
    grad_up = (grad_hidden * gate * gate_sig).astype(jnp.bfloat16)
    grad_w_gate = inner_rows(normed_two, grad_gate)
    grad_w_up = inner_rows(normed_two, grad_up)
    grad_normed_two = lax.psum(
        (outer_cols(grad_gate, gate_full) + outer_cols(grad_up, up_full)).astype(jnp.bfloat16), "tp"
    ).astype(jnp.float32)
    gain_two = jnp.sum(grad_normed_two * residual * scale_two, axis=0)
    effect_two = grad_normed_two * norm2_gain
    grad_resid = (
        out_grad.astype(jnp.float32)
        + scale_two * effect_two
        - residual
        * (scale_two * scale_two * scale_two)
        * jnp.mean(effect_two * residual, axis=-1, keepdims=True)
    )
    grad_resid_low = grad_resid.astype(jnp.bfloat16)
    grad_w_out = inner_rows(mixed_heads, grad_resid_low)
    grad_mixed = (
        outer_cols(grad_resid_low, out_full).astype(jnp.bfloat16).reshape(row_count, head_count, HD)
    )
    grad_sorted = arrange(grad_mixed, order)
    grad_split = regroup(grad_sorted, row_count)
    all_keys, all_values = (
        lax.all_gather(key_rows, "seq", axis=0, tiled=True),
        lax.all_gather(value_sorted, "seq", axis=0, tiled=True),
    )
    key_stack = all_keys.reshape(shard_count, row_count, head_count, HD)
    value_stack = all_values.reshape(shard_count, row_count, head_count, HD)
    kpos_stack = every_pos.reshape(shard_count, row_count)

    def back_step(grad_query, blocks):
        key_block, value_block, key_pos = blocks
        key_split = regroup(key_block, row_count)
        attn_weights, grad_score = split_grads(
            query_split,
            key_split,
            regroup(value_block, row_count),
            grad_split,
            qpos_split,
            regroup(key_pos, row_count),
            score_scale,
            score_bias,
        )
        grad_query = (
            grad_query
            + unsplit(
                jnp.einsum(
                    "shqk,skhd->sqhd", grad_score, key_split, preferred_element_type=jnp.float32
                )
            )
            * score_scale
        )
        key_term = (
            jnp.einsum(
                "shqk,sqhd->skhd", grad_score, query_split, preferred_element_type=jnp.float32
            )
            * score_scale
        )
        value_term = jnp.einsum(
            "shqk,sqhd->skhd", attn_weights, grad_split, preferred_element_type=jnp.float32
        )
        half_rows = row_count // 2
        key_back = jnp.swapaxes(key_term.reshape(2, 1, half_rows, head_cols), 0, 1).reshape(
            row_count, head_cols
        )
        value_back = jnp.swapaxes(value_term.reshape(2, 1, half_rows, head_cols), 0, 1).reshape(
            row_count, head_cols
        )
        return (grad_query, (key_back, value_back))

    grad_query, term_stack = lax.scan(back_step, zero_out, (key_stack, value_stack, kpos_stack))
    key_terms = term_stack[0].reshape(shard_count * row_count, head_cols)
    value_terms = term_stack[1].reshape(shard_count * row_count, head_cols)
    key_sum, value_sum = (
        lax.psum_scatter(
            key_terms.astype(jnp.bfloat16), "seq", scatter_dimension=0, tiled=True
        ).astype(jnp.float32),
        lax.psum_scatter(
            value_terms.astype(jnp.bfloat16), "seq", scatter_dimension=0, tiled=True
        ).astype(jnp.float32),
    )
    grad_query = arrange(grad_query, inverse)
    key_sum = arrange(key_sum, inverse)
    value_sum = arrange(value_sum, inverse)
    grad_query_lin = (
        rotate_back(grad_query, rot_cos, rot_sin).reshape(row_count, head_cols).astype(jnp.bfloat16)
    )
    grad_key_lin = (
        rotate_back(key_sum.reshape(row_count, head_count, HD), rot_cos, rot_sin)
        .reshape(row_count, head_cols)
        .astype(jnp.bfloat16)
    )
    grad_value_low = value_sum.astype(jnp.bfloat16)
    grad_w_query = inner_rows(normed_one, grad_query_lin)
    grad_w_key = inner_rows(normed_one, grad_key_lin)
    grad_w_value = inner_rows(normed_one, grad_value_low)
    grad_normed_one = lax.psum(
        (
            outer_cols(grad_query_lin, query_full)
            + outer_cols(grad_key_lin, key_full)
            + outer_cols(grad_value_low, value_full)
        ).astype(jnp.bfloat16),
        "tp",
    ).astype(jnp.float32)
    gain_one = jnp.sum(grad_normed_one * inputs * scale_one, axis=0)
    effect_one = grad_normed_one * norm1_gain
    in_grad = (
        grad_resid
        + scale_one * effect_one
        - inputs
        * (scale_one * scale_one * scale_one)
        * jnp.mean(effect_one * inputs, axis=-1, keepdims=True)
    )
    summed = (
        lax.psum_scatter(
            grad_w_query.astype(jnp.bfloat16), "seq", scatter_dimension=0, tiled=True
        ).astype(jnp.float32),
        lax.psum_scatter(
            grad_w_key.astype(jnp.bfloat16), "seq", scatter_dimension=0, tiled=True
        ).astype(jnp.float32),
        lax.psum_scatter(
            grad_w_value.astype(jnp.bfloat16), "seq", scatter_dimension=0, tiled=True
        ).astype(jnp.float32),
        lax.psum_scatter(
            grad_w_out.astype(jnp.bfloat16), "seq", scatter_dimension=1, tiled=True
        ).astype(jnp.float32),
        lax.psum_scatter(
            grad_w_gate.astype(jnp.bfloat16), "seq", scatter_dimension=0, tiled=True
        ).astype(jnp.float32),
        lax.psum_scatter(
            grad_w_up.astype(jnp.bfloat16), "seq", scatter_dimension=0, tiled=True
        ).astype(jnp.float32),
        lax.psum_scatter(
            grad_w_down.astype(jnp.bfloat16), "seq", scatter_dimension=1, tiled=True
        ).astype(jnp.float32),
        lax.psum_scatter(
            gain_one.astype(jnp.bfloat16), "seq", scatter_dimension=0, tiled=True
        ).astype(jnp.float32),
        lax.psum_scatter(
            gain_two.astype(jnp.bfloat16), "seq", scatter_dimension=0, tiled=True
        ).astype(jnp.float32),
    )
    return (
        layer_out,
        in_grad,
        summed[7],
        summed[8],
        summed[0],
        summed[1],
        summed[2],
        summed[3],
        summed[4],
        summed[5],
        summed[6],
    )


def solution(mesh):
    in_specs = (
        P("seq", None),
        P("seq"),
        P("seq"),
        P(),
        P(),
        P("seq", "tp"),
        P("seq", "tp"),
        P("seq", "tp"),
        P("tp", "seq"),
        P("seq", "tp"),
        P("seq", "tp"),
        P("tp", "seq"),
        P("seq", None),
    )
    out_specs = (
        P("seq", None),
        P("seq", None),
        P("seq"),
        P("seq"),
        P("seq", "tp"),
        P("seq", "tp"),
        P("seq", "tp"),
        P("tp", "seq"),
        P("seq", "tp"),
        P("seq", "tp"),
        P("tp", "seq"),
    )
    return jax.shard_map(
        on_device, mesh=mesh, in_specs=in_specs, out_specs=out_specs, check_vma=False
    )
```

profile of v0, /device:TPU:0, one launch (start us, length us, event | category | flops | bytes accessed | tf_op | source)
XLA Modules:
  0.0 1521.6 jit_solution(15668812939216227215)
XLA Ops:
  16.8 25.2 %all-gather.17.cloned.1.call-done = bf16[2048,512]{1,0:T(8,128)(2,1)} async-done(((bf16[256,512]{1,0:T(8,128)(2,1)}), bf16[2048,512]{1,0:T(8,128)(2,1)}) %all-gather.17.cloned.1.call-update) | async-done | bytes 2097168 | tf_op jit(solution)/shard_map/all_gather | solution.py:138
  45.0 27.8 %all-gather.15.cloned.1.call-done = bf16[2048,512]{1,0:T(8,128)(2,1)} async-done(((bf16[256,512]{1,0:T(8,128)(2,1)}), bf16[2048,512]{1,0:T(8,128)(2,1)}) %all-gather.15.cloned.1.call-update) | async-done | bytes 2097168 | tf_op jit(solution)/shard_map/all_gather | solution.py:137
  79.1 24.5 %all-gather.11.cloned.1.call-done = bf16[2048,512]{1,0:T(8,128)(2,1)} async-done(((bf16[256,512]{1,0:T(8,128)(2,1)}), bf16[2048,512]{1,0:T(8,128)(2,1)}) %all-gather.11.cloned.1.call-update) | async-done | bytes 2097168 | tf_op jit(solution)/shard_map/all_gather | solution.py:139
  112.6 13.4 all-gather
  132.0 20.4 %all-gather.19.cloned.1.call-done = bf16[4096,512]{0,1:T(8,128)(2,1)} async-done(((bf16[512,512]{0,1:T(8,128)(2,1)}), bf16[4096,512]{0,1:T(8,128)(2,1)}) %all-gather.19.cloned.1.call-update) | async-done | bytes 4194320 | tf_op jit(solution)/shard_map/all_gather | solution.py:164
  160.2 11.8 copy.119
  177.3 23.2 %all-gather.13.cloned.1.call-done = bf16[4096,512]{0,1:T(8,128)(2,1)} async-done(((bf16[512,512]{0,1:T(8,128)(2,1)}), bf16[4096,512]{0,1:T(8,128)(2,1)}) %all-gather.13.cloned.1.call-update) | async-done | bytes 4194320 | tf_op jit(solution)/shard_map/all_gather | solution.py:165
  208.2 11.8 copy.117
  262.3 94.0 %all-reduce.8.cloned.1.call-done = f32[512,2048]{1,0:T(8,128)} async-done(((f32[512,2048]{1,0:T(8,128)}), f32[512,2048]{1,0:T(8,128)}) %all-reduce.8.cloned.1.call-update) | async-done | bytes 4194320 | tf_op jit(solution)/shard_map/psum | solution.py:180
  361.6 79.1 %all-gather.23.cloned.1.call-done = bf16[2048,2048]{1,0:T(8,128)(2,1)} async-done(((bf16[256,2048]{1,0:T(8,128)(2,1)}), bf16[2048,2048]{1,0:T(8,128)(2,1)}) %all-gather.23.cloned.1.call-update) | async-done | bytes 8388624 | tf_op jit(solution)/shard_map/all_gather | solution.py:141
  450.0 73.5 %all-gather.25.cloned.1.call-done = bf16[2048,2048]{1,0:T(8,128)(2,1)} async-done(((bf16[256,2048]{1,0:T(8,128)(2,1)}), bf16[2048,2048]{1,0:T(8,128)(2,1)}) %all-gather.25.cloned.1.call-update) | async-done | bytes 8388624 | tf_op jit(solution)/shard_map/all_gather | solution.py:142
  532.9 73.7 %all-gather.27.cloned.1.call-done = bf16[2048,2048]{1,0:T(8,128)(2,1)} async-done(((bf16[2048,256]{1,0:T(8,128)(2,1)}), bf16[2048,2048]{1,0:T(8,128)(2,1)}) %all-gather.27.cloned.1.call-update) | async-done | bytes 8388624 | tf_op jit(solution)/shard_map/all_gather | solution.py:143
  662.7 38.2 %all-reduce.10.cloned.1.call-done = bf16[512,2048]{1,0:T(8,128)(2,1)} async-done(((bf16[512,2048]{1,0:T(8,128)(2,1)}), bf16[512,2048]{1,0:T(8,128)(2,1)}) %all-reduce.10.cloned.1.call-update) | async-done | bytes 2097168 | tf_op jit(solution)/shard_map/psum | solution.py:208
  711.9 172.8 %while.16 = (s32[]{:T(128)}, f32[512,4,128]{2,0,1:T(8,128)}, bf16[8,512,512]{2,1,0:T(8,128)(2,1)}, bf16[8,512,512]{2,1,0:T(8,128)(2,1)}, bf16[8,512,4,128]{3,1,2...) while((s32[]{:T(128)}, f32[512,4,128]{2,0,1:T(8,128)}, ...), condition=%wide.wide.region_9.10_spmd.clone, body=%wide.wide.region_8.9_spmd.clone.sunk | while | flops 678297600 | bytes 37630664 | solution.py:275
  892.3 42.6 %reduce-scatter.10.cloned.1.call-done = bf16[512,512]{1,0:T(8,128)(2,1)} async-done(((bf16[4096,512]{1,0:T(8,128)(2,1)}), bf16[512,512]{1,0:T(8,128)(2,1)}) %reduce-scatter.10.cloned.1.call-update) | async-done | bytes 524304 | tf_op jit(solution)/shard_map/reduce_scatter | solution.py:279
  951.3 34.1 %reduce-scatter.12.cloned.1.call-done = bf16[512,512]{1,0:T(8,128)(2,1)} async-done(((bf16[4096,512]{1,0:T(8,128)(2,1)}), bf16[512,512]{1,0:T(8,128)(2,1)}) %reduce-scatter.12.cloned.1.call-update) | async-done | bytes 524304 | tf_op jit(solution)/shard_map/reduce_scatter | solution.py:282
  1042.1 16.6 %reduce-scatter.14.cloned.1.call-done = bf16[256,512]{1,0:T(8,128)(2,1)} async-done(((bf16[2048,512]{1,0:T(8,128)(2,1)}), bf16[256,512]{1,0:T(8,128)(2,1)}) %reduce-scatter.14.cloned.1.call-update) | async-done | bytes 262160 | tf_op jit(solution)/shard_map/reduce_scatter | solution.py:319
  1060.5 34.7 %reduce-scatter.16.cloned.1.call-done = bf16[256,512]{1,0:T(8,128)(2,1)} async-done(((bf16[2048,512]{1,0:T(8,128)(2,1)}), bf16[256,512]{1,0:T(8,128)(2,1)}) %reduce-scatter.16.cloned.1.call-update) | async-done | bytes 262160 | tf_op jit(solution)/shard_map/reduce_scatter | solution.py:322
  1097.1 34.9 %reduce-scatter.18.cloned.1.call-done = bf16[256,512]{1,0:T(8,128)(2,1)} async-done(((bf16[2048,512]{1,0:T(8,128)(2,1)}), bf16[256,512]{1,0:T(8,128)(2,1)}) %reduce-scatter.18.cloned.1.call-update) | async-done | bytes 262160 | tf_op jit(solution)/shard_map/reduce_scatter | solution.py:325
  1133.8 105.0 %all-reduce.12.cloned.1.call-done = (bf16[512,2048]{1,0:T(8,128)(2,1)}, bf16[512,2048]{1,0:T(8,128)(2,1)}) async-done(((bf16[512,2048]{1,0:T(8,128)(2,1)}, bf16[512,2048]{1,0:T(8,128)(2,1)}), (bf16[512,2048]{1,0:T(8,128)(2,1)}, bf16[512,2048]{1,0:T(8,128)(2,1)})) %all-reduce.12.cloned.1.call-update) | async-done | bytes 4194320 | tf_op jit(solution)/shard_map/psum | solution.py:189
  1241.9 17.2 %all-reduce.2 = (bf16[2048]{0:T(1024)(128)(2,1)S(1)}, bf16[2048]{0:T(1024)(128)(2,1)S(1)}) all-reduce(bf16[2048]{0:T(1024)(128)(2,1)S(1)} %get-tuple-element.137, bf16[2048]{0:T(1024)(128)(2,1)S(1)} %get-tuple-element.135), channel_id=4, replica_groups=mesh['seq'=8,'tp'=4] {'seq'}, use_global_device_ids=true, to_apply=%region_15.16.clone | all-reduce | flops 4096 | bytes 16384
  1268.8 62.6 %reduce-scatter.22.cloned.1.call-done = bf16[256,2048]{1,0:T(8,128)(2,1)} async-done(((bf16[2048,2048]{1,0:T(8,128)(2,1)}), bf16[256,2048]{1,0:T(8,128)(2,1)}) %reduce-scatter.22.cloned.1.call-update) | async-done | bytes 1048592 | tf_op jit(solution)/shard_map/reduce_scatter | solution.py:331
  1334.1 87.3 %reduce-scatter.24.cloned.1.call-done = bf16[256,2048]{1,0:T(8,128)(2,1)} async-done(((bf16[2048,2048]{1,0:T(8,128)(2,1)}), bf16[256,2048]{1,0:T(8,128)(2,1)}) %reduce-scatter.24.cloned.1.call-update) | async-done | bytes 1048592 | tf_op jit(solution)/shard_map/reduce_scatter | solution.py:334
  1424.2 87.6 %reduce-scatter.26.cloned.1.call-done = bf16[2048,256]{1,0:T(8,128)(2,1)} async-done(((bf16[2048,2048]{1,0:T(8,128)(2,1)}), bf16[2048,256]{1,0:T(8,128)(2,1)}) %reduce-scatter.26.cloned.1.call-update) | async-done | bytes 1048592 | tf_op jit(solution)/shard_map/reduce_scatter | solution.py:337
  (410 shorter events, 465.6 us)
Async XLA Ops:
  7.2 34.8 %all-gather.17.cloned.1.call-start = ((), (), s32[]{:S(2)}) async-start(), calls=%async_computation.12 | async-start | bytes 2359296 | tf_op jit(solution)/shard_map/all_gather | solution.py:138
  9.2 63.7 %all-gather.15.cloned.1.call-start = ((), (), s32[]{:S(2)}) async-start(), calls=%async_computation.11 | async-start | bytes 2359296 | tf_op jit(solution)/shard_map/all_gather | solution.py:137
  11.0 92.6 %all-gather.11.cloned.1.call-start = ((), (), s32[]{:S(2)}) async-start(), calls=%async_computation.9 | async-start | bytes 2359296 | tf_op jit(solution)/shard_map/all_gather | solution.py:139
  12.9 139.5 %all-gather.19.cloned.1.call-start = ((), (), s32[]{:S(2)}) async-start(), calls=%async_computation.13 | async-start | bytes 4718592 | tf_op jit(solution)/shard_map/all_gather | solution.py:164
  79.1 121.3 %all-gather.13.cloned.1.call-start = ((), (), s32[]{:S(2)}) async-start(), calls=%async_computation.10 | async-start | bytes 4718592 | tf_op jit(solution)/shard_map/all_gather | solution.py:165
  110.1 138.4 %all-gather.21.cloned.1.call-start = ((), (), s32[]{:S(2)}) async-start(), calls=%async_computation.14 | async-start | bytes 2359296 | tf_op jit(solution)/shard_map/all_gather | solution.py:140
  111.9 244.4 %all-reduce.8.cloned.1.call-start = ((), (), s32[]{:S(2)}) async-start(), calls=%async_computation.15 | async-start | bytes 8388608 | tf_op jit(solution)/shard_map/psum | solution.py:180
  112.5 520.4 %copy-start.28 = (s32[4,128]{1,0:T(4,128)}, s32[4,128]{1,0:T(4,128)S(1)}, u32[]{:S(2)}) copy-start(s32[4,128]{1,0:T(4,128)S(1)} %gather_fusion.1) | copy-start | bytes 6148
  253.5 187.1 %all-gather.23.cloned.1.call-start = ((), (), s32[]{:S(2)}) async-start(), calls=%async_computation.16 | async-start | bytes 9437184 | tf_op jit(solution)/shard_map/all_gather | solution.py:141
  256.3 267.2 %all-gather.25.cloned.1.call-start = ((), (), s32[]{:S(2)}) async-start(), calls=%async_computation.17 | async-start | bytes 9437184 | tf_op jit(solution)/shard_map/all_gather | solution.py:142
  259.3 347.4 %all-gather.27.cloned.1.call-start = ((), (), s32[]{:S(2)}) async-start(), calls=%async_computation.18 | async-start | bytes 9437184 | tf_op jit(solution)/shard_map/all_gather | solution.py:143
  262.0 99.1 %copy-start.27 = (f32[2048]{0:T(1024)S(1)}, f32[2048]{0:T(1024)}, u32[]{:S(2)}) copy-start(f32[2048]{0:T(1024)} %param.19) | copy-start | bytes 24580
  262.1 438.8 %all-reduce.10.cloned.1.call-start = ((), (), s32[]{:S(2)}) async-start(), calls=%async_computation.19 | async-start | bytes 4194304 | tf_op jit(solution)/shard_map/psum | solution.py:208
  361.5 162.0 %copy-start.12 = (bf16[512,2048]{1,0:T(8,128)(2,1)}, bf16[512,2048]{1,0:T(8,128)(2,1)S(1)}, u32[]{:S(2)}) copy-start(bf16[512,2048]{1,0:T(8,128)(2,1)S(1)} %multiply_convert_fusion.3) | copy-start | bytes 6291460
  632.8 302.1 %reduce-scatter.10.cloned.1.call-start = ((), (), s32[]{:S(2)}) async-start(), calls=%async_computation.20 | async-start | bytes 4718592 | tf_op jit(solution)/shard_map/reduce_scatter | solution.py:279
  884.7 100.7 %reduce-scatter.12.cloned.1.call-start = ((), (), s32[]{:S(2)}) async-start(), calls=%async_computation.21 | async-start | bytes 4718592 | tf_op jit(solution)/shard_map/reduce_scatter | solution.py:282
  885.5 154.9 %reduce-scatter.20.cloned.1.call-start = ((), (), s32[]{:S(2)}) async-start(), calls=%async_computation.25 | async-start | bytes 2359296 | tf_op jit(solution)/shard_map/reduce_scatter | solution.py:328
  890.7 168.0 %reduce-scatter.14.cloned.1.call-start = ((), (), s32[]{:S(2)}) async-start(), calls=%async_computation.22 | async-start | bytes 2359296 | tf_op jit(solution)/shard_map/reduce_scatter | solution.py:319
  948.3 147.0 %reduce-scatter.16.cloned.1.call-start = ((), (), s32[]{:S(2)}) async-start(), calls=%async_computation.23 | async-start | bytes 2359296 | tf_op jit(solution)/shard_map/reduce_scatter | solution.py:322
  951.2 180.8 %reduce-scatter.18.cloned.1.call-start = ((), (), s32[]{:S(2)}) async-start(), calls=%async_computation.24 | async-start | bytes 2359296 | tf_op jit(solution)/shard_map/reduce_scatter | solution.py:325
  991.6 247.2 %all-reduce.12.cloned.1.call-start = ((), (), s32[]{:S(2)}) async-start(), calls=%async_computation.29 | async-start | bytes 8388608 | tf_op jit(solution)/shard_map/psum | solution.py:189
  1007.7 323.7 %reduce-scatter.22.cloned.1.call-start = ((), (), s32[]{:S(2)}) async-start(), calls=%async_computation.26 | async-start | bytes 9437184 | tf_op jit(solution)/shard_map/reduce_scatter | solution.py:331
  1017.9 403.5 %reduce-scatter.24.cloned.1.call-start = ((), (), s32[]{:S(2)}) async-start(), calls=%async_computation.27 | async-start | bytes 9437184 | tf_op jit(solution)/shard_map/reduce_scatter | solution.py:334
  1028.2 483.6 %reduce-scatter.26.cloned.1.call-start = ((), (), s32[]{:S(2)}) async-start(), calls=%async_computation.28 | async-start | bytes 9437184 | tf_op jit(solution)/shard_map/reduce_scatter | solution.py:337
  (49 other events, 520.0 us)
Sparse Core Ops, SparseCore 0:
  10.2 31.7 all-gather.16
  44.2 28.5 all-gather.14
  75.0 28.5 all-gather.10
  105.7 46.6 all-gather.18
  154.4 45.9 all-gather.12
  202.4 29.5 all-gather.20
  253.7 102.5 all-reduce.7
  358.5 82.0 all-gather.22
  442.9 80.5 all-gather.24
  525.6 81.0 all-gather.26
  633.0 67.8 all-reduce.9
  884.8 50.0 reduce-scatter.9
  937.2 48.1 reduce-scatter.11
  987.5 33.9 reduce-scatter.19
  1024.3 34.4 reduce-scatter.13
  1060.9 34.3 reduce-scatter.15
  1097.4 34.5 reduce-scatter.17
  1135.9 102.8 all-reduce.11
  1241.2 90.1 reduce-scatter.21
  1333.6 87.7 reduce-scatter.23
  1423.8 87.9 reduce-scatter.25
where the time goes:
time: 1530 us; the launch traced here: 1520 us
  waiting for transfers between devices  986 us (64%)
  local copies, waits for them, and re-layouts  210 us (14%)
  matrix products  195 us (13%)
  other arithmetic  81.9 us (5%)
  blocking collectives  30.6 us (2%)
  between operations  15.9 us (1%)
    psum x1, waiting for transfers between devices, on_device(): lax.psum(matrix(hidden, down_full).astype(jnp.bfloat16), 'tp')  105 us
    psum x1, waiting for transfers between devices, on_device(): residual = inputs + lax.psum(matrix(mixed_heads, out_full), 'tp')  94 us
    reduce_scatter x1, waiting for transfers between devices, on_device(): lax.psum_scatter(grad_w_down.astype(jnp.bfloat16), 'seq', scatter_dimensi...  87.6 us
    reduce_scatter x1, waiting for transfers between devices, on_device(): lax.psum_scatter(grad_w_up.astype(jnp.bfloat16), 'seq', scatter_dimension...  87.3 us
    all_gather x1, waiting for transfers between devices, on_device(): lax.all_gather(w_gate.astype(jnp.bfloat16), 'seq', axis=0, tiled=True)  79.1 us
    all_gather x1, waiting for transfers between devices, on_device(): lax.all_gather(w_down.astype(jnp.bfloat16), 'seq', axis=1, tiled=True)  73.7 us
    all_gather x1, waiting for transfers between devices, on_device(): lax.all_gather(w_up.astype(jnp.bfloat16), 'seq', axis=0, tiled=True)  73.5 us
    reduce_scatter x1, waiting for transfers between devices, on_device(): lax.psum_scatter(grad_w_gate.astype(jnp.bfloat16), 'seq', scatter_dimensi...  62.6 us
  transfers between devices with their start and end apart: 21, of which 19 were waited for; matrix products, arithmetic and copies ran while one was open for 17% of the time, Pallas kernels for 0%

commit v1 on v0

--- a/solution.py
+++ b/solution.py
@@ -161,8 +161,13 @@
     query_split = regroup(query_sorted, row_count)
     qpos_split = regroup(pos_sorted, row_count)
     zero_out = jnp.zeros((row_count, head_count, HD), jnp.float32)
-    key_block = lax.all_gather(key_rows, "seq", axis=0, tiled=True)
-    value_block = lax.all_gather(value_sorted, "seq", axis=0, tiled=True)
+    key_block, value_block = jnp.split(
+        lax.all_gather(
+            jnp.concatenate([key_rows, value_sorted], axis=1), "seq", axis=0, tiled=True
+        ),
+        [key_rows.shape[1]],
+        axis=1,
+    )
     piece_rows = key_block.shape[0]
     key_pos = every_pos
     key_heads_piece = key_block.reshape(piece_rows, head_count, HD)

time: 1530 us -> 1630 us (1.065)
  waiting for transfers between devices: 986 us -> 1070 us
    all_gather x2 -> x3, waiting for transfers between devices: 43.5 us -> 108 us  [the longest x1 54.3 us: on_device(): lax.all_gather(jnp.concatenate([key_rows, value_sorted], axis=1), 'seq',...]
    psum x1, waiting for transfers between devices: 38.2 us -> 57.9 us  [on_device(): lax.psum((outer_cols(grad_gate, gate_full) + outer_cols(grad_up, up_full)...]
  transfers between devices with their start and end apart: 21 -> 22, of which waited for: 19 -> 20; matrix products, arithmetic and copies ran while one was open for 17% -> 18% of each run, Pallas kernels for 0% -> 0%
where the time goes in v1:
time: 1630 us; the launch traced here: 1620 us
  waiting for transfers between devices  1070 us (66%)
  local copies, waits for them, and re-layouts  219 us (13%)
  matrix products  194 us (12%)
  other arithmetic  84.4 us (5%)
  blocking collectives  30.7 us (2%)
    psum x1, waiting for transfers between devices, on_device(): lax.psum(matrix(hidden, down_full).astype(jnp.bfloat16), 'tp')  105 us
    psum x1, waiting for transfers between devices, on_device(): residual = inputs + lax.psum(matrix(mixed_heads, out_full), 'tp')  92.2 us
    reduce_scatter x1, waiting for transfers between devices, on_device(): lax.psum_scatter(grad_w_down.astype(jnp.bfloat16), 'seq', scatter_dimensi...  87.6 us
    reduce_scatter x1, waiting for transfers between devices, on_device(): lax.psum_scatter(grad_w_up.astype(jnp.bfloat16), 'seq', scatter_dimension...  87.4 us
    all_gather x1, waiting for transfers between devices, on_device(): lax.all_gather(w_gate.astype(jnp.bfloat16), 'seq', axis=0, tiled=True)  79.1 us
    all_gather x1, waiting for transfers between devices, on_device(): lax.all_gather(w_down.astype(jnp.bfloat16), 'seq', axis=1, tiled=True)  73.9 us
    all_gather x1, waiting for transfers between devices, on_device(): lax.all_gather(w_up.astype(jnp.bfloat16), 'seq', axis=0, tiled=True)  73.5 us
    reduce_scatter x1, waiting for transfers between devices, on_device(): lax.psum_scatter(grad_w_gate.astype(jnp.bfloat16), 'seq', scatter_dimensi...  62.4 us
  transfers between devices with their start and end apart: 22, of which 20 were waited for; matrix products, arithmetic and copies ran while one was open for 18% of the time, Pallas kernels for 0%

profile of v1, /device:TPU:0, one launch (start us, length us, event | category | flops | bytes accessed | tf_op | source)
XLA Modules:
  0.0 1618.0 jit_solution(8736320568862244404)
XLA Ops:
  16.9 25.2 %all-gather.12.cloned.1.call-done = bf16[2048,512]{1,0:T(8,128)(2,1)} async-done(((bf16[256,512]{1,0:T(8,128)(2,1)}), bf16[2048,512]{1,0:T(8,128)(2,1)}) %all-gather.12.cloned.1.call-update) | async-done | bytes 2097168 | tf_op jit(solution)/shard_map/all_gather | solution.py:138
  45.0 27.8 %all-gather.18.cloned.1.call-done = bf16[2048,512]{1,0:T(8,128)(2,1)} async-done(((bf16[256,512]{1,0:T(8,128)(2,1)}), bf16[2048,512]{1,0:T(8,128)(2,1)}) %all-gather.18.cloned.1.call-update) | async-done | bytes 2097168 | tf_op jit(solution)/shard_map/all_gather | solution.py:137
  78.3 25.4 %all-gather.14.cloned.1.call-done = bf16[2048,512]{1,0:T(8,128)(2,1)} async-done(((bf16[256,512]{1,0:T(8,128)(2,1)}), bf16[2048,512]{1,0:T(8,128)(2,1)}) %all-gather.14.cloned.1.call-update) | async-done | bytes 2097168 | tf_op jit(solution)/shard_map/all_gather | solution.py:139
  112.9 13.4 all-gather
  137.8 54.3 %all-gather.16.cloned.1.call-done = bf16[4096,1024]{0,1:T(8,128)(2,1)} async-done(((bf16[512,1024]{0,1:T(8,128)(2,1)}), bf16[4096,1024]{0,1:T(8,128)(2,1)}) %all-gather.16.cloned.1.call-update) | async-done | bytes 8388624 | tf_op jit(solution)/shard_map/all_gather | solution.py:165
  206.0 11.8 copy.120
  286.6 92.2 %all-reduce.8.cloned.1.call-done = f32[512,2048]{1,0:T(8,128)} async-done(((f32[512,2048]{1,0:T(8,128)}), f32[512,2048]{1,0:T(8,128)}) %all-reduce.8.cloned.1.call-update) | async-done | bytes 4194320 | tf_op jit(solution)/shard_map/psum | solution.py:185
  384.1 79.1 %all-gather.22.cloned.1.call-done = bf16[2048,2048]{1,0:T(8,128)(2,1)} async-done(((bf16[256,2048]{1,0:T(8,128)(2,1)}), bf16[2048,2048]{1,0:T(8,128)(2,1)}) %all-gather.22.cloned.1.call-update) | async-done | bytes 8388624 | tf_op jit(solution)/shard_map/all_gather | solution.py:141
  472.6 73.5 %all-gather.24.cloned.1.call-done = bf16[2048,2048]{1,0:T(8,128)(2,1)} async-done(((bf16[256,2048]{1,0:T(8,128)(2,1)}), bf16[2048,2048]{1,0:T(8,128)(2,1)}) %all-gather.24.cloned.1.call-update) | async-done | bytes 8388624 | tf_op jit(solution)/shard_map/all_gather | solution.py:142
  555.5 73.9 %all-gather.26.cloned.1.call-done = bf16[2048,2048]{1,0:T(8,128)(2,1)} async-done(((bf16[2048,256]{1,0:T(8,128)(2,1)}), bf16[2048,2048]{1,0:T(8,128)(2,1)}) %all-gather.26.cloned.1.call-update) | async-done | bytes 8388624 | tf_op jit(solution)/shard_map/all_gather | solution.py:143
  656.5 20.4 %all-gather.28.cloned.1.call-done = bf16[4096,512]{0,1:T(8,128)(2,1)} async-done(((bf16[512,512]{0,1:T(8,128)(2,1)}), bf16[4096,512]{0,1:T(8,128)(2,1)}) %all-gather.28.cloned.1.call-update) | async-done | bytes 4194320 | tf_op jit(solution)/shard_map/all_gather | solution.py:233
  691.5 33.6 %all-gather.30.cloned.1.call-done = bf16[4096,512]{0,1:T(8,128)(2,1)} async-done(((bf16[512,512]{0,1:T(8,128)(2,1)}), bf16[4096,512]{0,1:T(8,128)(2,1)}) %all-gather.30.cloned.1.call-update) | async-done | bytes 4194320 | tf_op jit(solution)/shard_map/all_gather | solution.py:234
  739.5 57.9 %all-reduce.10.cloned.1.call-done = bf16[512,2048]{1,0:T(8,128)(2,1)} async-done(((bf16[512,2048]{1,0:T(8,128)(2,1)}), bf16[512,2048]{1,0:T(8,128)(2,1)}) %all-reduce.10.cloned.1.call-update) | async-done | bytes 2097168 | tf_op jit(solution)/shard_map/psum | solution.py:213
  808.4 172.8 %while.16 = (s32[]{:T(128)}, f32[512,4,128]{2,0,1:T(8,128)}, bf16[8,512,512]{2,1,0:T(8,128)(2,1)}, bf16[8,512,512]{2,1,0:T(8,128)(2,1)}, bf16[8,512,4,128]{3,1,2...) while((s32[]{:T(128)}, f32[512,4,128]{2,0,1:T(8,128)}, ...), condition=%wide.wide.region_9.10_spmd.clone, body=%wide.wide.region_8.9_spmd.clone.sunk | while | flops 678297600 | bytes 37630664 | solution.py:280
  988.6 42.8 %reduce-scatter.10.cloned.1.call-done = bf16[512,512]{1,0:T(8,128)(2,1)} async-done(((bf16[4096,512]{1,0:T(8,128)(2,1)}), bf16[512,512]{1,0:T(8,128)(2,1)}) %reduce-scatter.10.cloned.1.call-update) | async-done | bytes 524304 | tf_op jit(solution)/shard_map/reduce_scatter | solution.py:284
  1047.7 34.0 %reduce-scatter.12.cloned.1.call-done = bf16[512,512]{1,0:T(8,128)(2,1)} async-done(((bf16[4096,512]{1,0:T(8,128)(2,1)}), bf16[512,512]{1,0:T(8,128)(2,1)}) %reduce-scatter.12.cloned.1.call-update) | async-done | bytes 524304 | tf_op jit(solution)/shard_map/reduce_scatter | solution.py:287
  1138.5 16.5 %reduce-scatter.14.cloned.1.call-done = bf16[256,512]{1,0:T(8,128)(2,1)} async-done(((bf16[2048,512]{1,0:T(8,128)(2,1)}), bf16[256,512]{1,0:T(8,128)(2,1)}) %reduce-scatter.14.cloned.1.call-update) | async-done | bytes 262160 | tf_op jit(solution)/shard_map/reduce_scatter | solution.py:324
  1156.7 34.8 %reduce-scatter.16.cloned.1.call-done = bf16[256,512]{1,0:T(8,128)(2,1)} async-done(((bf16[2048,512]{1,0:T(8,128)(2,1)}), bf16[256,512]{1,0:T(8,128)(2,1)}) %reduce-scatter.16.cloned.1.call-update) | async-done | bytes 262160 | tf_op jit(solution)/shard_map/reduce_scatter | solution.py:327
  1193.3 34.9 %reduce-scatter.18.cloned.1.call-done = bf16[256,512]{1,0:T(8,128)(2,1)} async-done(((bf16[2048,512]{1,0:T(8,128)(2,1)}), bf16[256,512]{1,0:T(8,128)(2,1)}) %reduce-scatter.18.cloned.1.call-update) | async-done | bytes 262160 | tf_op jit(solution)/shard_map/reduce_scatter | solution.py:330
  1230.0 105.1 %all-reduce.12.cloned.1.call-done = (bf16[512,2048]{1,0:T(8,128)(2,1)}, bf16[512,2048]{1,0:T(8,128)(2,1)}) async-done(((bf16[512,2048]{1,0:T(8,128)(2,1)}, bf16[512,2048]{1,0:T(8,128)(2,1)}), (bf16[512,2048]{1,0:T(8,128)(2,1)}, bf16[512,2048]{1,0:T(8,128)(2,1)})) %all-reduce.12.cloned.1.call-update) | async-done | bytes 4194320 | tf_op jit(solution)/shard_map/psum | solution.py:194
  1338.3 17.3 %all-reduce.2 = (bf16[2048]{0:T(1024)(128)(2,1)S(1)}, bf16[2048]{0:T(1024)(128)(2,1)S(1)}) all-reduce(bf16[2048]{0:T(1024)(128)(2,1)S(1)} %get-tuple-element.137, bf16[2048]{0:T(1024)(128)(2,1)S(1)} %get-tuple-element.135), channel_id=4, replica_groups=mesh['seq'=8,'tp'=4] {'seq'}, use_global_device_ids=true, to_apply=%region_15.16.clone | all-reduce | flops 4096 | bytes 16384
  1365.2 62.4 %reduce-scatter.22.cloned.1.call-done = bf16[256,2048]{1,0:T(8,128)(2,1)} async-done(((bf16[2048,2048]{1,0:T(8,128)(2,1)}), bf16[256,2048]{1,0:T(8,128)(2,1)}) %reduce-scatter.22.cloned.1.call-update) | async-done | bytes 1048592 | tf_op jit(solution)/shard_map/reduce_scatter | solution.py:336
  1430.4 87.4 %reduce-scatter.24.cloned.1.call-done = bf16[256,2048]{1,0:T(8,128)(2,1)} async-done(((bf16[2048,2048]{1,0:T(8,128)(2,1)}), bf16[256,2048]{1,0:T(8,128)(2,1)}) %reduce-scatter.24.cloned.1.call-update) | async-done | bytes 1048592 | tf_op jit(solution)/shard_map/reduce_scatter | solution.py:339
  1520.6 87.6 %reduce-scatter.26.cloned.1.call-done = bf16[2048,256]{1,0:T(8,128)(2,1)} async-done(((bf16[2048,2048]{1,0:T(8,128)(2,1)}), bf16[2048,256]{1,0:T(8,128)(2,1)}) %reduce-scatter.26.cloned.1.call-update) | async-done | bytes 1048592 | tf_op jit(solution)/shard_map/reduce_scatter | solution.py:342
  (415 shorter events, 490.1 us)
Async XLA Ops:
  7.2 34.8 %all-gather.12.cloned.1.call-start = ((), (), s32[]{:S(2)}) async-start(), calls=%async_computation.9 | async-start | bytes 2359296 | tf_op jit(solution)/shard_map/all_gather | solution.py:138
  9.2 63.7 %all-gather.18.cloned.1.call-start = ((), (), s32[]{:S(2)}) async-start(), calls=%async_computation.12 | async-start | bytes 2359296 | tf_op jit(solution)/shard_map/all_gather | solution.py:137
  11.0 92.6 %all-gather.14.cloned.1.call-start = ((), (), s32[]{:S(2)}) async-start(), calls=%async_computation.10 | async-start | bytes 2359296 | tf_op jit(solution)/shard_map/all_gather | solution.py:139
  12.9 179.2 %all-gather.16.cloned.1.call-start = ((), (), s32[]{:S(2)}) async-start(), calls=%async_computation.11 | async-start | bytes 9437184 | tf_op jit(solution)/shard_map/all_gather | solution.py:165
  110.4 160.9 %all-gather.20.cloned.1.call-start = ((), (), s32[]{:S(2)}) async-start(), calls=%async_computation.13 | async-start | bytes 2359296 | tf_op jit(solution)/shard_map/all_gather | solution.py:140
  112.2 266.7 %all-reduce.8.cloned.1.call-start = ((), (), s32[]{:S(2)}) async-start(), calls=%async_computation.14 | async-start | bytes 8388608 | tf_op jit(solution)/shard_map/psum | solution.py:185
  112.8 542.8 %copy-start.28 = (s32[4,128]{1,0:T(4,128)}, s32[4,128]{1,0:T(4,128)S(1)}, u32[]{:S(2)}) copy-start(s32[4,128]{1,0:T(4,128)S(1)} %gather_fusion.2) | copy-start | bytes 6148
  276.4 186.9 %all-gather.22.cloned.1.call-start = ((), (), s32[]{:S(2)}) async-start(), calls=%async_computation.15 | async-start | bytes 9437184 | tf_op jit(solution)/shard_map/all_gather | solution.py:141
  279.2 267.0 %all-gather.24.cloned.1.call-start = ((), (), s32[]{:S(2)}) async-start(), calls=%async_computation.16 | async-start | bytes 9437184 | tf_op jit(solution)/shard_map/all_gather | solution.py:142
  282.4 347.1 %all-gather.26.cloned.1.call-start = ((), (), s32[]{:S(2)}) async-start(), calls=%async_computation.17 | async-start | bytes 9437184 | tf_op jit(solution)/shard_map/all_gather | solution.py:143
  285.1 391.8 %all-gather.28.cloned.1.call-start = ((), (), s32[]{:S(2)}) async-start(), calls=%async_computation.19 | async-start | bytes 4718592 | tf_op jit(solution)/shard_map/all_gather | solution.py:233
  285.7 439.4 %all-gather.30.cloned.1.call-start = ((), (), s32[]{:S(2)}) async-start(), calls=%async_computation.20 | async-start | bytes 4718592 | tf_op jit(solution)/shard_map/all_gather | solution.py:234
  286.4 510.9 %all-reduce.10.cloned.1.call-start = ((), (), s32[]{:S(2)}) async-start(), calls=%async_computation.18 | async-start | bytes 4194304 | tf_op jit(solution)/shard_map/psum | solution.py:213
  384.1 162.0 %copy-start.14 = (bf16[512,2048]{1,0:T(8,128)(2,1)}, bf16[512,2048]{1,0:T(8,128)(2,1)S(1)}, u32[]{:S(2)}) copy-start(bf16[512,2048]{1,0:T(8,128)(2,1)S(1)} %multiply_convert_fusion.3) | copy-start | bytes 6291460
  655.6 375.8 %reduce-scatter.10.cloned.1.call-start = ((), (), s32[]{:S(2)}) async-start(), calls=%async_computation.21 | async-start | bytes 4718592 | tf_op jit(solution)/shard_map/reduce_scatter | solution.py:284
  981.2 100.5 %reduce-scatter.12.cloned.1.call-start = ((), (), s32[]{:S(2)}) async-start(), calls=%async_computation.22 | async-start | bytes 4718592 | tf_op jit(solution)/shard_map/reduce_scatter | solution.py:287
  981.8 154.9 %reduce-scatter.20.cloned.1.call-start = ((), (), s32[]{:S(2)}) async-start(), calls=%async_computation.26 | async-start | bytes 2359296 | tf_op jit(solution)/shard_map/reduce_scatter | solution.py:333
  987.0 167.9 %reduce-scatter.14.cloned.1.call-start = ((), (), s32[]{:S(2)}) async-start(), calls=%async_computation.23 | async-start | bytes 2359296 | tf_op jit(solution)/shard_map/reduce_scatter | solution.py:324
  1044.8 146.7 %reduce-scatter.16.cloned.1.call-start = ((), (), s32[]{:S(2)}) async-start(), calls=%async_computation.24 | async-start | bytes 2359296 | tf_op jit(solution)/shard_map/reduce_scatter | solution.py:327
  1047.7 180.5 %reduce-scatter.18.cloned.1.call-start = ((), (), s32[]{:S(2)}) async-start(), calls=%async_computation.25 | async-start | bytes 2359296 | tf_op jit(solution)/shard_map/reduce_scatter | solution.py:330
  1087.9 247.3 %all-reduce.12.cloned.1.call-start = ((), (), s32[]{:S(2)}) async-start(), calls=%async_computation.30 | async-start | bytes 8388608 | tf_op jit(solution)/shard_map/psum | solution.py:194
  1104.0 323.6 %reduce-scatter.22.cloned.1.call-start = ((), (), s32[]{:S(2)}) async-start(), calls=%async_computation.27 | async-start | bytes 9437184 | tf_op jit(solution)/shard_map/reduce_scatter | solution.py:336
  1114.2 403.6 %reduce-scatter.24.cloned.1.call-start = ((), (), s32[]{:S(2)}) async-start(), calls=%async_computation.28 | async-start | bytes 9437184 | tf_op jit(solution)/shard_map/reduce_scatter | solution.py:339
  1124.6 483.6 %reduce-scatter.26.cloned.1.call-start = ((), (), s32[]{:S(2)}) async-start(), calls=%async_computation.29 | async-start | bytes 9437184 | tf_op jit(solution)/shard_map/reduce_scatter | solution.py:342
  (50 other events, 622.9 us)
Sparse Core Ops, SparseCore 0:
  10.2 31.7 all-gather.11
  44.2 28.5 all-gather.17
  75.0 28.5 all-gather.13
  110.5 81.5 all-gather.15
  194.1 29.3 all-gather.19
  276.5 102.3 all-reduce.7
  381.1 82.0 all-gather.21
  465.5 80.5 all-gather.23
  548.4 81.0 all-gather.25
  631.5 45.3 all-gather.27
  679.2 45.8 all-gather.29
  728.9 68.3 all-reduce.9
  981.3 49.9 reduce-scatter.9
  1033.5 48.1 reduce-scatter.11
  1083.8 34.0 reduce-scatter.19
  1120.6 34.2 reduce-scatter.13
  1157.1 34.4 reduce-scatter.15
  1193.7 34.5 reduce-scatter.17
  1232.3 102.8 all-reduce.11
  1337.4 90.1 reduce-scatter.21
  1430.0 87.7 reduce-scatter.23
  1520.2 87.9 reduce-scatter.25
